TPU v7x, 128 devices: a whole 4x4x4 slice. The times are simulated.
128 devices in a mesh: row: 8 (over z, core), col: 16 (over y, x).
Axes of the slice: x: 4, y: 4, z: 4, core: 2. Of those that a mesh axis runs over, the one named last changes fastest.
Arguments:
- panel_blocks: bfloat16 [16, 8, 512, 512], P('col', None, 'row'), may hold values from -0.25 to 0.25
- factor_inverse: bfloat16 [16, 512, 512], P('col')
- target_rows: int32 [16, 8], replicated, may hold values from 0 to 15, as said below
- owner_order: int32 [16], replicated, may hold values from 0 to 15, each once
- ancestor_rows: float32 [16, 512, 8192], P('col', 'row'), may hold values from -1.8 to 1.8
Outputs:
- updated_rows: float32 [16, 512, 8192], P('col', 'row')
Inputs may be any that keep to these rules, and one draw needn't show every extreme that they name: `target_rows`: each row names 8 different ancestor block rows in ascending order; each index of col holds exactly one supernode. `owner_order`: each ancestor block row once.
All inputs are finite; a program needn't handle non-finite values.
Results may differ from a plain program's by a relative error of at most 0.0024.
Values may be sent and summed in bfloat16 or wider, within the bound.
A program may use at most 192 MiB of HBM per device.

v0:
```python
import jax
import jax.numpy as jnp
from jax import lax
from jax.sharding import PartitionSpec as P


def body(panel_blocks, factor_inverse, target_rows, owner_order, ancestor_rows):
    col_size = lax.axis_size("col")
    width = panel_blocks.shape[3]
    ancestors = owner_order.shape[0]
    col_place = lax.axis_index("col")
    own_targets = lax.dynamic_slice_in_dim(target_rows, col_place, 1, 0)[0]
    own_solved = jnp.einsum(
        "piw,vw->piv", panel_blocks[0], factor_inverse[0], preferred_element_type=jnp.float32
    ).astype(jnp.bfloat16)
    full_solved = lax.all_gather(own_solved, "row", axis=1, tiled=True)
    products = jnp.einsum(
        "piw,qmw->piqm", own_solved, full_solved, preferred_element_type=jnp.float32
    ).astype(jnp.bfloat16)
    matched = own_targets[None, :] == owner_order[:, None]
    places = lax.broadcasted_iota(jnp.int32, matched.shape, 1)
    position = jnp.sum(jnp.where(matched, places, 0), axis=1)
    present = jnp.any(matched, axis=1)
    send = jnp.where(
        present[:, None, None, None], products[position], jnp.zeros((), products.dtype)
    )
    received = lax.all_to_all(send, "col", 0, 0, tiled=True)
    block_ids = lax.broadcasted_iota(jnp.int32, (1, 1, ancestors), 2)
    onehot = (target_rows[:, :, None] == block_ids).astype(jnp.bfloat16)
    update = jnp.einsum("sqb,siqm->ibm", onehot, received, preferred_element_type=jnp.float32)
    return ancestor_rows - update.reshape(ancestor_rows.shape)


def solution(mesh):
    return jax.shard_map(
        body,
        mesh=mesh,
        in_specs=(
            P("col", None, "row", None),
            P("col", None, None),
            P(),
            P(),
            P("col", "row", None),
        ),
        out_specs=P("col", "row", None),
        check_vma=False,
    )
```

profile of v0, /device:TPU:1, one launch (start us, length us, event | category | flops | bytes accessed | tf_op | source)
XLA Modules:
  0.0 218.7 jit_solution(13225717698894345203)
XLA Ops:
  6.5 0.0 copy-start
  6.5 0.0 all-gather.2.cloned.1.call-start
  6.5 1.0 copy-done
  7.6 2.3 %convolution_convert_fusion = bf16[8,64,512]{2,1,0:T(8,128)(2,1)} fusion(bf16[1,512,512]{2,1,0:T(8,128)(2,1)S(1)} %copy-done, bf16[1,8,64,512]{3,2,1,0:T(8,128)(2,1)} %param.5), kind=kOutput, calls=%fused_computation.6 | convolution fusion | flops 268697600 | bytes 1572864 | tf_op jit(solution)/shard_map/piw,vw->piv/dot_general | solution.py:13
  9.9 0.0 all-gather.2.cloned.1.call-update
  9.9 0.9 dynamic-slice_reduce_fusion
  10.8 0.7 fusion.11
  11.5 0.7 compare_reduce_fusion
  12.3 33.7 %all-gather.2.cloned.1.call-done = bf16[8,512,512]{2,1,0:T(8,128)(2,1)} async-done(((bf16[8,64,512]{2,1,0:T(8,128)(2,1)}), bf16[8,512,512]{2,1,0:T(8,128)(2,1)}) %all-gather.2.cloned.1.call-update) | async-done | bytes 4194320 | tf_op jit(solution)/shard_map/all_gather | solution.py:16
  46.0 4.7 %fusion.2 = bf16[8,64,8,512]{3,1,2,0:T(8,128)(2,1)S(1)} fusion(bf16[8,512,512]{2,1,0:T(8,128)(2,1)} %all-gather.2.cloned.1.call-done, bf16[8,64,512]{2,1,0:T(8,128)(2,1)} %convolution_convert_fusion), kind=kOutput, calls=%fused_computation.4 | convolution fusion | flops 2149580800 | bytes 8912896 | tf_op jit(solution)/shard_map/piw,qmw->piqm/dot_general | solution.py:17
  50.8 4.5 %copy.9 = bf16[8,64,8,512]{3,2,1,0:T(8,128)(2,1)} copy(bf16[8,64,8,512]{3,1,2,0:T(8,128)(2,1)S(1)} %fusion.2) | data formatting | bytes 8388608 | tf_op jit(solution)/shard_map/convert_element_type | solution.py:19
  55.2 6.9 %gather_fusion = bf16[16,64,8,512]{3,2,1,0:T(8,128)(2,1)} fusion(bf16[8,64,8,512]{3,2,1,0:T(8,128)(2,1)} %copy.9, s32[1024]{0:T(1024)S(1)} %pad_clamp_fusion), kind=kCustom, calls=%fused_computation | custom fusion | bytes 16777280 | tf_op jit(solution)/shard_map/gather | solution.py:25
  62.1 7.2 %broadcast_select_fusion = bf16[16,64,8,512]{3,2,1,0:T(8,128)(2,1)} fusion(bf16[16,64,8,512]{3,2,1,0:T(8,128)(2,1)} %gather_fusion, pred[16]{0:T(512)(128)(4,1)S(1)} %compare_reduce_fusion), kind=kLoop, calls=%fused_computation.1 | loop fusion | flops 4194304 | bytes 16777232 | tf_op jit(solution)/shard_map/jit(_where)/select_n | solution.py:24
  69.3 0.0 copy-start.1
  69.3 6.7 %all-to-all-start = ((bf16[16,64,8,512]{3,2,1,0:T(8,128)(2,1)}), bf16[16,64,8,512]{3,2,1,0:T(8,128)(2,1)}, u32[]{:S(2)}, u32[]{:S(2)}) async-start(bf16[16,64,8,512]{3,2,1,0:T(8,128)(2,1)} %broadcast_select_fusion), calls=%async_computation | async-start | bytes 16777216 | tf_op jit(solution)/shard_map/all_to_all | solution.py:27
  76.0 0.0 copy-done.1
  76.0 0.1 copy.10
  76.1 124.9 %all-to-all-done = bf16[16,64,8,512]{3,2,1,0:T(8,128)(2,1)} async-done(((bf16[16,64,8,512]{3,2,1,0:T(8,128)(2,1)}), bf16[16,64,8,512]{3,2,1,0:T(8,128)(2,1)}, u32[]{:S(2)}, u32[]{:S(2)}) %all-to-all-start) | async-done | bytes 8388640 | tf_op jit(solution)/shard_map/all_to_all | solution.py:27
  201.0 6.0 %convolution_bitcast_fusion = f32[64,16,512]{2,1,0:T(8,128)} fusion(bf16[16,64,8,512]{3,2,1,0:T(8,128)(2,1)} %all-to-all-done, s32[16,8]{1,0:T(8,128)S(1)} %copy.10), kind=kOutput, calls=%fused_computation.5 | convolution fusion | flops 134219776 | bytes 10486272 | tf_op jit(solution)/shard_map/sqb,siqm->ibm/dot_general | solution.py:30
  207.0 1.7 reshape.19
  208.7 3.1 %sub.3 = f32[1,64,8192]{2,1,0:T(8,128)} subtract(f32[1,64,8192]{2,1,0:T(8,128)} %param.9, f32[1,64,8192]{2,1,0:T(8,128)S(1)} %reshape.19) | non-fusion elementwise | flops 524288 | bytes 6291456 | tf_op jit(solution)/shard_map/sub | solution.py:31
  (2 shorter events, 0.0 us)
Async XLA Ops:
  6.5 1.0 copy-start
  6.5 39.5 %all-gather.2.cloned.1.call-start = ((), (), s32[]{:S(2)}) async-start(), calls=%async_computation.1 | async-start | bytes 4718592 | tf_op jit(solution)/shard_map/all_gather | solution.py:16
  69.3 6.7 %copy-start.1 = (s32[16,8]{0,1:T(8,128)S(1)}, s32[16,8]{0,1:T(8,128)}, u32[]{:S(2)}) copy-start(s32[16,8]{0,1:T(8,128)} %param.7) | copy-start | bytes 1540
  69.3 131.7 %all-to-all-start = ((bf16[16,64,8,512]{3,2,1,0:T(8,128)(2,1)}), bf16[16,64,8,512]{3,2,1,0:T(8,128)(2,1)}, u32[]{:S(2)}, u32[]{:S(2)}) async-start(bf16[16,64,8,512]{3,2,1,0:T(8,128)(2,1)} %broadcast_select_fusion), calls=%async_computation | async-start | bytes 16777216 | tf_op jit(solution)/shard_map/all_to_all | solution.py:27
Sparse Core Ops, SparseCore 0:
  10.0 35.9 all-gather.1
where the time goes:
time: 219 us
  waiting for transfers between devices  159 us (73%)
  local copies, waits for them, and re-layouts  15.1 us (7%)
  between operations  13.4 us (6%)
  matrix products  13 us (6%)
  other arithmetic  11.8 us (5%)
  starting transfers between devices  6.71 us (3%)
    all_to_all x1, waiting for transfers between devices, body(): received = lax.all_to_all(send, 'col', 0, 0, tiled=True)  125 us
    all_gather x1, waiting for transfers between devices, body(): full_solved = lax.all_gather(own_solved, 'row', axis=1, tiled=True)  33.7 us
    select_n x1, other arithmetic, body(): jnp.where(present[:, None, None, None], products[position], jnp.zeros((),...  7.2 us
    gather x1, local copies, waits for them, and re-layouts, body(): products[position]  6.87 us
    all_to_all x1, starting transfers between devices, body(): received = lax.all_to_all(send, 'col', 0, 0, tiled=True)  6.71 us
    dot_general x1, matrix products, body(): jnp.einsum('sqb,siqm->ibm', onehot, received, preferred_element_type=jnp....  6.02 us
    dot_general x1, matrix products, body(): jnp.einsum('piw,qmw->piqm', own_solved, full_solved, preferred_element_ty...  4.73 us
    convert_element_type x1, local copies, waits for them, and re-layouts, body(): products = jnp.einsum('piw,qmw->piqm', own_solved, full_solved, preferred...  4.47 us
  transfers between devices with their start and end apart: 2, of which 2 were waited for; matrix products, arithmetic and copies ran while one was open for 1% of the time, Pallas kernels for 0%

commit v1 on v0

--- a/solution.py
+++ b/solution.py
@@ -2,6 +2,12 @@
 import jax.numpy as jnp
 from jax import lax
 from jax.sharding import PartitionSpec as P
+
+
+def in_order(parts, dim):
+    parts = jnp.moveaxis(parts, 0, dim)
+    shape = parts.shape
+    return parts.reshape(*shape[:dim], shape[dim] * shape[dim + 1], *shape[dim + 2 :])
 
 
 def body(panel_blocks, factor_inverse, target_rows, owner_order, ancestor_rows):
@@ -13,7 +19,19 @@
     own_solved = jnp.einsum(
         "piw,vw->piv", panel_blocks[0], factor_inverse[0], preferred_element_type=jnp.float32
     ).astype(jnp.bfloat16)
-    full_solved = lax.all_gather(own_solved, "row", axis=1, tiled=True)
+    size = lax.axis_size("row")
+    pairs = [(i, (i + 1) % size) for i in range(size)]
+    back = [(b, a) for a, b in pairs]
+    lower, upper = ([], [])
+    for hop in range(size - 1):
+        if hop % 2 == 0:
+            lower.append(lax.ppermute(lower[-1] if lower else own_solved, "row", pairs))
+        else:
+            upper.append(lax.ppermute(upper[-1] if upper else own_solved, "row", back))
+    tiles = jnp.stack([*lower[::-1], own_solved, *upper])
+    shift = lax.axis_index("row") - len(lower)
+    tiles = tiles[(jnp.arange(size) - shift) % size]
+    full_solved = in_order(tiles, 1)
     products = jnp.einsum(
         "piw,qmw->piqm", own_solved, full_solved, preferred_element_type=jnp.float32
     ).astype(jnp.bfloat16)

time: 219 us -> 220 us (level)
  the two profiles are of different devices: /device:TPU:1 before, /device:TPU:97 now
where the time goes in v1:
time: 220 us
  waiting for transfers between devices  150 us (68%)
  local copies, waits for them, and re-layouts  29.3 us (13%)
  starting transfers between devices  18 us (8%)
  other arithmetic  11.9 us (5%)
  matrix products  10 us (5%)
    all_to_all x1, waiting for transfers between devices, body(): received = lax.all_to_all(send, 'col', 0, 0, tiled=True)  128 us
    ppermute x4, waiting for transfers between devices, body(): lower.append(lax.ppermute(lower[-1] if lower else own_solved, 'row', pairs))  21.2 us
    ppermute x4, starting transfers between devices, body(): lower.append(lax.ppermute(lower[-1] if lower else own_solved, 'row', pairs))  11.1 us
    select_n x1, other arithmetic, body(): jnp.where(present[:, None, None, None], products[position], jnp.zeros((),...  7.22 us
    unnamed x12, local copies, waits for them, and re-layouts  7.01 us
    all_to_all x1, starting transfers between devices, body(): received = lax.all_to_all(send, 'col', 0, 0, tiled=True)  6.93 us
    gather x1, local copies, waits for them, and re-layouts, body(): products[position]  6.88 us
    dot_general x1, matrix products, body(): jnp.einsum('sqb,siqm->ibm', onehot, received, preferred_element_type=jnp....  6.02 us
  transfers between devices with their start and end apart: 8, of which 6 were waited for; matrix products, arithmetic and copies ran while one was open for 4% of the time, Pallas kernels for 0%

profile of v1, /device:TPU:97, one launch (start us, length us, event | category | flops | bytes accessed | tf_op | source)
XLA Modules:
  0.0 219.7 jit_solution(12683726123276447445)
XLA Ops:
  0.0 1.0 copy-done
  1.0 1.5 convolution_convert_fusion.1
  2.6 6.1 %collective-permute-done = bf16[8,64,512]{2,1,0:T(8,128)(2,1)S(1)} collective-permute-done((bf16[8,64,512]{2,1,0:T(8,128)(2,1)S(1)}, bf16[8,64,512]{2,1,0:T(8,128)(2,1)S(1)}, u32[]{:S(2)}, u32[]{:S(2)}) %collective-permute-start) | collective-permute-done | bytes 524320 | tf_op jit(solution)/shard_map/ppermute | solution.py:28
  8.7 3.7 %collective-permute-start.1 = (bf16[8,64,512]{2,1,0:T(8,128)(2,1)S(1)}, bf16[8,64,512]{2,1,0:T(8,128)(2,1)S(1)}, u32[]{:S(2)}, u32[]{:S(2)}) collective-permute-start(bf16[8,64,512]{2,1,0:T(8,128)(2,1)S(1)} %collective-permute-done), channel_id=1, source_target_pairs={{0,16},{16,32},{32,48},{48,64},{64,80},{80,96},{96,112},{112,0},{1... | collective-permute-start | bytes 1572872 | tf_op jit(solution)/shard_map/ppermute | solution.py:28
  12.4 6.1 %collective-permute-done.1 = bf16[8,64,512]{2,1,0:T(8,128)(2,1)S(1)} collective-permute-done((bf16[8,64,512]{2,1,0:T(8,128)(2,1)S(1)}, bf16[8,64,512]{2,1,0:T(8,128)(2,1)S(1)}, u32[]{:S(2)}, u32[]{:S(2)}) %collective-permute-start.1) | collective-permute-done | bytes 524320 | tf_op jit(solution)/shard_map/ppermute | solution.py:28
  18.5 3.7 %collective-permute-start.2 = (bf16[8,64,512]{2,1,0:T(8,128)(2,1)S(1)}, bf16[8,64,512]{2,1,0:T(8,128)(2,1)S(1)}, u32[]{:S(2)}, u32[]{:S(2)}) collective-permute-start(bf16[8,64,512]{2,1,0:T(8,128)(2,1)S(1)} %collective-permute-done.1), channel_id=1, source_target_pairs={{0,16},{16,32},{32,48},{48,64},{64,80},{80,96},{96,112},{112,0},{1... | collective-permute-start | bytes 1572872 | tf_op jit(solution)/shard_map/ppermute | solution.py:28
  22.2 0.9 dynamic-slice_reduce_fusion
  23.1 0.7 fusion.6
  23.9 4.5 %collective-permute-done.2 = bf16[8,64,512]{2,1,0:T(8,128)(2,1)S(1)} collective-permute-done((bf16[8,64,512]{2,1,0:T(8,128)(2,1)S(1)}, bf16[8,64,512]{2,1,0:T(8,128)(2,1)S(1)}, u32[]{:S(2)}, u32[]{:S(2)}) %collective-permute-start.2) | collective-permute-done | bytes 524320 | tf_op jit(solution)/shard_map/ppermute | solution.py:28
  28.3 3.7 %collective-permute-start.3 = (bf16[8,64,512]{2,1,0:T(8,128)(2,1)S(1)}, bf16[8,64,512]{2,1,0:T(8,128)(2,1)S(1)}, u32[]{:S(2)}, u32[]{:S(2)}) collective-permute-start(bf16[8,64,512]{2,1,0:T(8,128)(2,1)S(1)} %collective-permute-done.2), channel_id=1, source_target_pairs={{0,16},{16,32},{32,48},{48,64},{64,80},{80,96},{96,112},{112,0},{1... | collective-permute-start | bytes 1572872 | tf_op jit(solution)/shard_map/ppermute | solution.py:28
  32.1 0.7 compare_reduce_fusion
  32.8 0.9 collective-permute-done.5
  33.7 4.5 %collective-permute-done.3 = bf16[8,64,512]{2,1,0:T(8,128)(2,1)S(1)} collective-permute-done((bf16[8,64,512]{2,1,0:T(8,128)(2,1)S(1)}, bf16[8,64,512]{2,1,0:T(8,128)(2,1)S(1)}, u32[]{:S(2)}, u32[]{:S(2)}) %collective-permute-start.3) | collective-permute-done | bytes 524320 | tf_op jit(solution)/shard_map/ppermute | solution.py:28
  38.2 0.8 bitcast_dynamic-update-slice_fusion.7
  39.0 0.8 bitcast_dynamic-update-slice_fusion.6
  39.8 0.9 bitcast_dynamic-update-slice_fusion.5
  40.7 0.9 bitcast_dynamic-update-slice_fusion.4
  41.5 0.8 bitcast_dynamic-update-slice_fusion.3
  42.4 0.9 bitcast_dynamic-update-slice_fusion.2
  43.2 0.8 bitcast_dynamic-update-slice_fusion.1
  44.1 0.8 bitcast_dynamic-update-slice_fusion
  44.9 5.0 %gather_fusion = bf16[8,8,64,512]{3,2,1,0:T(8,128)(2,1)} fusion(bf16[8,8,64,512]{3,2,1,0:T(8,128)(2,1)} %bitcast_dynamic-update-slice_fusion, s32[1024]{0:T(1024)S(1)} %pad_clamp_fusion.1), kind=kCustom, calls=%fused_computation | custom fusion | bytes 8388640 | tf_op jit(solution)/shard_map/gather | solution.py:33
  49.9 2.5 %copy.11 = bf16[8,8,64,512]{3,2,1,0:T(8,128)(2,1)S(1)} copy(bf16[8,8,64,512]{3,2,0,1:T(8,128)(2,1)} %bitcast.49) | data formatting | bytes 8388608 | tf_op jit(solution)/shard_map/transpose | solution.py:8
  52.3 2.5 %convolution_convert_fusion = bf16[8,64,8,512]{3,1,2,0:T(8,128)(2,1)S(1)} fusion(bf16[8,512,512,1]{2,1,0,3:T(8,128)(2,1)S(1)} %bitcast.50, bf16[8,64,512]{2,1,0:T(8,128)(2,1)S(1)} %convolution_convert_fusion.1), kind=kOutput, calls=%fused_computation.3 | convolution fusion | flops 2149580800 | bytes 8912896 | tf_op jit(solution)/shard_map/piw,qmw->piqm/dot_general | solution.py:35
  54.8 4.5 %copy.12 = bf16[8,64,8,512]{3,2,1,0:T(8,128)(2,1)} copy(bf16[8,64,8,512]{3,1,2,0:T(8,128)(2,1)S(1)} %convolution_convert_fusion) | data formatting | bytes 8388608 | tf_op jit(solution)/shard_map/convert_element_type | solution.py:37
  59.3 6.9 %gather_fusion.1 = bf16[16,64,8,512]{3,2,1,0:T(8,128)(2,1)} fusion(bf16[8,64,8,512]{3,2,1,0:T(8,128)(2,1)} %copy.12, s32[1024]{0:T(1024)S(1)} %pad_clamp_fusion), kind=kCustom, calls=%fused_computation.1 | custom fusion | bytes 16777280 | tf_op jit(solution)/shard_map/gather | solution.py:43
  66.2 7.2 %broadcast_select_fusion = bf16[16,64,8,512]{3,2,1,0:T(8,128)(2,1)} fusion(bf16[16,64,8,512]{3,2,1,0:T(8,128)(2,1)} %gather_fusion.1, pred[16]{0:T(512)(128)(4,1)S(1)} %compare_reduce_fusion), kind=kLoop, calls=%fused_computation.2 | loop fusion | flops 4194304 | bytes 16777232 | tf_op jit(solution)/shard_map/jit(_where)/select_n | solution.py:42
  73.4 6.9 %all-to-all-start = ((bf16[16,64,8,512]{3,2,1,0:T(8,128)(2,1)}), bf16[16,64,8,512]{3,2,1,0:T(8,128)(2,1)}, u32[]{:S(2)}, u32[]{:S(2)}) async-start(bf16[16,64,8,512]{3,2,1,0:T(8,128)(2,1)} %broadcast_select_fusion), calls=%async_computation | async-start | bytes 16777216 | tf_op jit(solution)/shard_map/all_to_all | solution.py:45
  80.4 128.4 %all-to-all-done = bf16[16,64,8,512]{3,2,1,0:T(8,128)(2,1)} async-done(((bf16[16,64,8,512]{3,2,1,0:T(8,128)(2,1)}), bf16[16,64,8,512]{3,2,1,0:T(8,128)(2,1)}, u32[]{:S(2)}, u32[]{:S(2)}) %all-to-all-start) | async-done | bytes 8388640 | tf_op jit(solution)/shard_map/all_to_all | solution.py:45
  208.8 6.0 %convolution_bitcast_fusion = f32[64,16,512]{2,1,0:T(8,128)} fusion(bf16[16,64,8,512]{3,2,1,0:T(8,128)(2,1)} %all-to-all-done, s32[16,8]{1,0:T(8,128)S(1)} %copy.13), kind=kOutput, calls=%fused_computation.4 | convolution fusion | flops 134219776 | bytes 10486272 | tf_op jit(solution)/shard_map/sqb,siqm->ibm/dot_general | solution.py:48
  214.8 1.7 reshape.72
  216.6 3.1 %sub.22 = f32[1,64,8192]{2,1,0:T(8,128)} subtract(f32[1,64,8192]{2,1,0:T(8,128)} %param.9, f32[1,64,8192]{2,1,0:T(8,128)S(1)} %reshape.72) | non-fusion elementwise | flops 524288 | bytes 6291456 | tf_op jit(solution)/shard_map/sub | solution.py:49
  (14 shorter events, 0.1 us)
Async XLA Ops:
  0.0 1.0 copy-start
  2.6 6.1 %collective-permute-start = (bf16[8,64,512]{2,1,0:T(8,128)(2,1)S(1)}, bf16[8,64,512]{2,1,0:T(8,128)(2,1)S(1)}, u32[]{:S(2)}, u32[]{:S(2)}) collective-permute-start(bf16[8,64,512]{2,1,0:T(8,128)(2,1)S(1)} %convolution_convert_fusion.1), channel_id=1, source_target_pairs={{0,16},{16,32},{32,48},{48,64},{64,80},{80,96},{96,112},{112,0},{1... | collective-permute-start | bytes 1572872 | tf_op jit(solution)/shard_map/ppermute | solution.py:28
  8.7 9.8 %collective-permute-start.1 = (bf16[8,64,512]{2,1,0:T(8,128)(2,1)S(1)}, bf16[8,64,512]{2,1,0:T(8,128)(2,1)S(1)}, u32[]{:S(2)}, u32[]{:S(2)}) collective-permute-start(bf16[8,64,512]{2,1,0:T(8,128)(2,1)S(1)} %collective-permute-done), channel_id=1, source_target_pairs={{0,16},{16,32},{32,48},{48,64},{64,80},{80,96},{96,112},{112,0},{1... | collective-permute-start | bytes 1572872 | tf_op jit(solution)/shard_map/ppermute | solution.py:28
  12.4 11.4 %collective-permute-start.4 = (bf16[8,64,512]{2,1,0:T(8,128)(2,1)S(1)}, bf16[8,64,512]{2,1,0:T(8,128)(2,1)S(1)}, u32[]{:S(2)}, u32[]{:S(2)}) collective-permute-start(bf16[8,64,512]{2,1,0:T(8,128)(2,1)S(1)} %convolution_convert_fusion.1), channel_id=1, source_target_pairs={{16,0},{32,16},{48,32},{64,48},{80,64},{96,80},{112,96},{0,112},{1... | collective-permute-start | bytes 1572872 | tf_op jit(solution)/shard_map/ppermute | solution.py:30
  18.5 9.8 %collective-permute-start.2 = (bf16[8,64,512]{2,1,0:T(8,128)(2,1)S(1)}, bf16[8,64,512]{2,1,0:T(8,128)(2,1)S(1)}, u32[]{:S(2)}, u32[]{:S(2)}) collective-permute-start(bf16[8,64,512]{2,1,0:T(8,128)(2,1)S(1)} %collective-permute-done.1), channel_id=1, source_target_pairs={{0,16},{16,32},{32,48},{48,64},{64,80},{80,96},{96,112},{112,0},{1... | collective-permute-start | bytes 1572872 | tf_op jit(solution)/shard_map/ppermute | solution.py:28
  23.8 9.8 %collective-permute-start.5 = (bf16[8,64,512]{2,1,0:T(8,128)(2,1)S(1)}, bf16[8,64,512]{2,1,0:T(8,128)(2,1)S(1)}, u32[]{:S(2)}, u32[]{:S(2)}) collective-permute-start(bf16[8,64,512]{2,1,0:T(8,128)(2,1)S(1)} %collective-permute-done.4), channel_id=1, source_target_pairs={{16,0},{32,16},{48,32},{64,48},{80,64},{96,80},{112,96},{0,112},{1... | collective-permute-start | bytes 1572872 | tf_op jit(solution)/shard_map/ppermute | solution.py:30
  28.3 9.8 %collective-permute-start.3 = (bf16[8,64,512]{2,1,0:T(8,128)(2,1)S(1)}, bf16[8,64,512]{2,1,0:T(8,128)(2,1)S(1)}, u32[]{:S(2)}, u32[]{:S(2)}) collective-permute-start(bf16[8,64,512]{2,1,0:T(8,128)(2,1)S(1)} %collective-permute-done.2), channel_id=1, source_target_pairs={{0,16},{16,32},{32,48},{48,64},{64,80},{80,96},{96,112},{112,0},{1... | collective-permute-start | bytes 1572872 | tf_op jit(solution)/shard_map/ppermute | solution.py:28
  33.7 10.4 %collective-permute-start.6 = (bf16[8,64,512]{2,1,0:T(8,128)(2,1)S(1)}, bf16[8,64,512]{2,1,0:T(8,128)(2,1)S(1)}, u32[]{:S(2)}, u32[]{:S(2)}) collective-permute-start(bf16[8,64,512]{2,1,0:T(8,128)(2,1)S(1)} %collective-permute-done.5), channel_id=1, source_target_pairs={{16,0},{32,16},{48,32},{64,48},{80,64},{96,80},{112,96},{0,112},{1... | collective-permute-start | bytes 1572872 | tf_op jit(solution)/shard_map/ppermute | solution.py:30
  73.4 6.9 %copy-start.1 = (s32[16,8]{0,1:T(8,128)S(1)}, s32[16,8]{0,1:T(8,128)}, u32[]{:S(2)}) copy-start(s32[16,8]{0,1:T(8,128)} %param.7) | copy-start | bytes 1540
  73.4 135.4 %all-to-all-start = ((bf16[16,64,8,512]{3,2,1,0:T(8,128)(2,1)}), bf16[16,64,8,512]{3,2,1,0:T(8,128)(2,1)}, u32[]{:S(2)}, u32[]{:S(2)}) async-start(bf16[16,64,8,512]{3,2,1,0:T(8,128)(2,1)} %broadcast_select_fusion), calls=%async_computation | async-start | bytes 16777216 | tf_op jit(solution)/shard_map/all_to_all | solution.py:45
